TPU v7x, 32 devices: a whole 2x2x4 slice. The times are simulated.
32 devices in a mesh: dp: 8 (over y, x, core), section: 4 (over z).
Axes of the slice: x: 2, y: 2, z: 4, core: 2. Of those that a mesh axis runs over, the one named last changes fastest.
Arguments:
- inputs: bfloat16 [1280, 8192], P('dp'), may hold values from -6 to 6
- cotangent: bfloat16 [1280, 8192], P('dp'), may hold values from -0.625 to 0.625
- weight_in: bfloat16 [4, 8192, 512], P('section'), may hold values from -0.0625 to 0.0625
- weight_out: bfloat16 [4, 8192, 512], P('section'), may hold values from -0.25 to 0.25
- norm_gains: float32 [4, 8192], P('section'), may hold values from 0.1 to 1.9
Outputs:
- in_grad: float32 [4, 8192, 512], P('section', 'dp')
- out_grad: float32 [4, 8192, 512], P('section', 'dp')
- gain_grad: float32 [4, 8192], P('section', 'dp')
All inputs are finite; a program needn't handle non-finite values.
Results may differ from a plain program's by a relative error of at most 0.025.
Values may be sent and summed in bfloat16 or wider, within the bound.
A program may use at most 192 MiB of HBM per device.

v0:
```python
import functools

import jax
import jax.numpy as jnp
from jax import lax
from jax.experimental import pallas as pl
from jax.experimental.pallas import tpu as pltpu
from jax.sharding import PartitionSpec as P

ROWS = 16
CHUNK = 4096
DELAY = 1
EPSILON = 1e-05
MESH = pl.DeviceIdType.MESH


def nt_dot(left, right):
    return lax.dot_general(
        left, right, (((1,), (1,)), ((), ())), preferred_element_type=jnp.float32
    )


def column_product(left, right):
    return lax.dot_general(
        left, right, (((0,), (0,)), ((), ())), preferred_element_type=jnp.float32
    )


def relay_kernel(
    sections,
    replicas,
    micros,
    x_ref,
    c_ref,
    win_hbm,
    wout_hbm,
    gain_ref,
    all_h,
    all_g,
    all_act,
    all_du,
    win,
    wout,
    stash,
    up,
    out_f,
    out_b,
    act_buf,
    du_buf,
    pre,
    scale,
    w_sem,
    f_recv,
    b_recv,
    f_send,
    b_send,
    x_recv,
    x_send,
):
    width = stash.shape[2]
    chunks = width // CHUNK
    pos = lax.axis_index("section")
    block = width // replicas
    me = lax.axis_index("dp")
    is_first = pos == 0
    is_last = pos == sections - 1
    not_first = pos > 0
    not_last = pos < sections - 1

    def cols(k):
        return pl.ds(pl.multiple_of(k * CHUNK, CHUNK), CHUNK)

    win_copy = pltpu.make_async_copy(win_hbm, win, w_sem.at[0])
    wout_copy = pltpu.make_async_copy(wout_hbm, wout, w_sem.at[1])
    win_copy.start()

    @pl.when(is_first)
    def _():
        @pl.loop(0, micros)
        def _(m):
            @pl.loop(0, chunks)
            def _(k):
                pltpu.make_async_copy(
                    x_ref.at[m, :, cols(k)], stash.at[m, :, cols(k)], f_recv.at[m, k]
                ).start()

    wout_copy.start()

    @pl.when(is_last)
    def _():
        @pl.loop(0, micros)
        def _(m):
            @pl.loop(0, chunks)
            def _(k):
                pltpu.make_async_copy(
                    c_ref.at[m, :, cols(k)], up.at[m, :, cols(k)], b_recv.at[m, k]
                ).start()

    barrier = pltpu.get_barrier_semaphore()

    @pl.when(not_first)
    def _():
        pl.semaphore_signal(
            barrier, inc=1, device_id={"section": pos - 1}, device_id_type=MESH
        )

    @pl.when(not_last)
    def _():
        pl.semaphore_signal(
            barrier, inc=1, device_id={"section": pos + 1}, device_id_type=MESH
        )

    @pl.loop(1, replicas)
    def _(step):
        pl.semaphore_signal(
            barrier,
            inc=1,
            device_id={"dp": lax.rem(me + step, replicas)},
            device_id_type=MESH,
        )

    pl.semaphore_wait(
        barrier,
        replicas - 1 + not_first.astype(jnp.int32) + not_last.astype(jnp.int32),
    )

    def send_forward(m, k):
        return pltpu.make_async_remote_copy(
            src_ref=out_f.at[m, :, cols(k)],
            dst_ref=stash.at[m, :, cols(k)],
            send_sem=f_send.at[m, k],
            recv_sem=f_recv.at[m, k],
            device_id={"section": pos + 1},
            device_id_type=MESH,
        )

    def send_backward(m, k):
        return pltpu.make_async_remote_copy(
            src_ref=out_b.at[m, :, cols(k)],
            dst_ref=up.at[m, :, cols(k)],
            send_sem=b_send.at[m, k],
            recv_sem=b_recv.at[m, k],
            device_id={"section": pos - 1},
            device_id_type=MESH,
        )

    def share(kind, src_of, dst):
        pltpu.make_async_copy(src_of(me), dst, x_recv.at[kind]).start()

        @pl.loop(1, replicas)
        def _(step):
            peer = lax.rem(me + step, replicas)
            pltpu.make_async_remote_copy(
                src_ref=src_of(peer),
                dst_ref=dst,
                send_sem=x_send.at[kind],
                recv_sem=x_recv.at[kind],
                device_id={"dp": peer},
                device_id_type=MESH,
            ).start()

    def part(owner):
        return pl.ds(pl.multiple_of(owner * block, block), block)

    def forward(m):
        @pl.when(m == 0)
        def _():
            win_copy.wait()

        def project(k, carry):
            total, acc = carry
            piece = stash.at[m, :, cols(k)]
            pltpu.make_async_copy(piece, piece, f_recv.at[m, k]).wait()
            h = stash[m, :, cols(k)].astype(jnp.float32)
            scaled = (h * gain_ref[:, cols(k)]).astype(jnp.bfloat16)
            return (
                total + jnp.sum(h * h, axis=1, keepdims=True),
                acc
                + jnp.dot(scaled, win[cols(k), :], preferred_element_type=jnp.float32),
            )

        total, u = lax.fori_loop(
            0,
            chunks,
            project,
            (
                jnp.zeros((ROWS, 1), jnp.float32),
                jnp.zeros((ROWS, win.shape[1]), jnp.float32),
            ),
        )
        inv = lax.rsqrt(total / width + EPSILON)
        u = u * inv
        act = (u * jax.nn.sigmoid(u)).astype(jnp.bfloat16)
        pre[m] = u
        scale[m] = jnp.broadcast_to(inv, scale.shape[1:])
        act_buf[m] = act

        @pl.when(m == 0)
        def _():
            wout_copy.wait()

        @pl.when(not_last)
        def _():
            @pl.loop(0, chunks)
            def _(k):
                h = stash[m, :, cols(k)].astype(jnp.float32)
                out_f[m, :, cols(k)] = (h + nt_dot(act, wout[cols(k), :])).astype(
                    jnp.bfloat16
                )
                send_forward(m, k).start()

        share(0, lambda owner: stash.at[m, :, part(owner)], all_h.at[me, m])
        share(1, lambda owner: act_buf.at[m], all_act.at[me, m])

    def backward(m):
        def project(k, acc):
            piece = up.at[m, :, cols(k)]
            pltpu.make_async_copy(piece, piece, b_recv.at[m, k]).wait()
            return acc + jnp.dot(
                up[m, :, cols(k)], wout[cols(k), :], preferred_element_type=jnp.float32
            )

        da = lax.fori_loop(
            0, chunks, project, jnp.zeros((ROWS, win.shape[1]), jnp.float32)
        )
        u = pre[m]
        inv = scale[m][:, :1]
        sig = jax.nn.sigmoid(u)
        wide_du = da * sig * (1.0 + u * (1.0 - sig))
        du = wide_du.astype(jnp.bfloat16)
        du_buf[m] = (wide_du * inv).astype(jnp.bfloat16)
        centered = jnp.sum(du.astype(jnp.float32) * u, axis=1, keepdims=True) / (
            inv * width
        )
        pull = inv * inv * inv * centered

        @pl.when(not_first)
        def _():
            @pl.loop(0, chunks)
            def _(k):
                h = stash[m, :, cols(k)].astype(jnp.float32)
                g = up[m, :, cols(k)].astype(jnp.float32)
                dn = nt_dot(du, win[cols(k), :])
                out_b[m, :, cols(k)] = (
                    g + inv * (dn * gain_ref[:, cols(k)]) - h * pull
                ).astype(jnp.bfloat16)
                send_backward(m, k).start()

        share(2, lambda owner: up.at[m, :, part(owner)], all_g.at[me, m])
        share(3, lambda owner: du_buf.at[m], all_du.at[me, m])

    @pl.loop(0, micros + 2 * DELAY * (sections - 1))
    def _(tick):
        mf = tick - DELAY * pos
        mb = tick - DELAY * (2 * (sections - 1) - pos)

        @pl.when((mf >= 0) & (mf < micros))
        def _():
            forward(mf)

        @pl.when((mb >= 0) & (mb < micros))
        def _():
            backward(mb)

    @pl.loop(0, micros)
    def _(m):
        @pl.loop(0, chunks)
        def _(k):
            @pl.when(not_last)
            def _():
                send_forward(m, k).wait_send()

            @pl.when(not_first)
            def _():
                send_backward(m, k).wait_send()

    for kind, ref in enumerate((all_h, all_act, all_g, all_du)):
        sent = ref.at[pl.ds(0, replicas - 1)]
        pltpu.make_async_copy(sent, sent, x_send.at[kind]).wait()
        pltpu.make_async_copy(ref, ref, x_recv.at[kind]).wait()


def local(sections, replicas, inputs, cotangent, weight_in, weight_out, norm_gains):
    tokens, width = inputs.shape
    hidden = weight_in.shape[2]
    micros = tokens // ROWS
    block = width // replicas
    wide = jax.ShapeDtypeStruct((replicas, micros, ROWS, block), jnp.bfloat16)
    narrow = jax.ShapeDtypeStruct((replicas, micros, ROWS, hidden), jnp.bfloat16)
    any_spec = pl.BlockSpec(memory_space=pl.ANY)
    vmem_spec = pl.BlockSpec(memory_space=pltpu.VMEM)
    wide_scratch = pltpu.VMEM((micros, ROWS, width), jnp.bfloat16)
    weight_scratch = pltpu.VMEM((width, hidden), jnp.bfloat16)
    dma = pltpu.SemaphoreType.DMA
    all_h, all_g, all_act, all_du = pl.pallas_call(
        functools.partial(relay_kernel, sections, replicas, micros),
        out_shape=(
            wide,
            wide,
            narrow,
            narrow,
        ),
        in_specs=[any_spec] * 4 + [vmem_spec],
        out_specs=(any_spec,) * 4,
        scratch_shapes=[
            weight_scratch,
            weight_scratch,
            wide_scratch,
            wide_scratch,
            wide_scratch,
            wide_scratch,
            pltpu.VMEM((micros, ROWS, hidden), jnp.bfloat16),
            pltpu.VMEM((micros, ROWS, hidden), jnp.bfloat16),
            pltpu.VMEM((micros, ROWS, hidden), jnp.float32),
            pltpu.VMEM((micros, ROWS, 128), jnp.float32),
            dma((2,)),
            dma((micros, width // CHUNK)),
            dma((micros, width // CHUNK)),
            dma((micros, width // CHUNK)),
            dma((micros, width // CHUNK)),
            dma((4,)),
            dma((4,)),
        ],
        compiler_params=pltpu.CompilerParams(
            collective_id=0, has_side_effects=True, vmem_limit_bytes=60 * 2**20
        ),
    )(
        inputs.reshape(micros, ROWS, width),
        cotangent.reshape(micros, ROWS, width),
        weight_in[0],
        weight_out[0],
        norm_gains,
    )
    total = replicas * tokens
    own = lax.axis_index("dp") * block
    own_gain = lax.dynamic_slice_in_dim(norm_gains[0], own, block, 0)
    own_rows = lax.dynamic_slice_in_dim(weight_in[0], own, block, 0)
    raw_grad = column_product(
        all_h.reshape(total, block), all_du.reshape(total, hidden)
    )
    in_grad = own_gain[:, None] * raw_grad
    gain_grad = jnp.sum(own_rows.astype(jnp.float32) * raw_grad, axis=1)
    out_grad = column_product(
        all_g.reshape(total, block), all_act.reshape(total, hidden)
    )
    return (in_grad[None], out_grad[None], gain_grad[None])


def solution(mesh):
    return jax.shard_map(
        functools.partial(local, mesh.shape["section"], mesh.shape["dp"]),
        mesh=mesh,
        in_specs=(
            P("dp", None),
            P("dp", None),
            P("section", None, None),
            P("section", None, None),
            P("section", None),
        ),
        out_specs=(P("section", "dp", None), P("section", "dp", None), P("section", "dp")),
        check_vma=False,
    )
```

profile of v0, /device:TPU:0, one launch (start us, length us, event | category | flops | bytes accessed | tf_op | source)
XLA Modules:
  0.0 148.0 jit_solution(9051774470019323773)
XLA Ops:
  0.6 0.7 constant_dynamic-slice_fusion.1
  1.3 1.3 constant_dynamic-slice_fusion
  2.6 0.5 copy.12
  3.2 133.8 %shard_map.76 = (bf16[8,10,16,1024]{3,2,1,0:T(8,128)(2,1)}, bf16[8,10,16,1024]{3,2,1,0:T(8,128)(2,1)}, bf16[8,10,16,512]{3,2,1,0:T(8,128)(2,1)}, bf16[8,10,16,512]{3,2,1,0:T(8,128)(2,1)}) custom-call(bf16[10,16,8192]{2,1,0:T(8,128)(2,1)} %bitcast.30, bf16[10,16,8192]{2,1,0:T(8,128)(2,1)} %bitcast.31, bf16[8192,512]{1,0:T(8,128)(2,1)} %bitcast.28, ...), custom_call_target="tpu_custom_call" | custom-call | tf_op jit(solution)/shard_map/pallas_call | solution.py:295
  137.0 4.3 %fusion = (f32[1024]{0:T(1024)}, f32[1,1024,512]{1,2,0:T(8,128)S(1)}) fusion(bf16[1,1024,512]{1,2,0:T(8,128)(2,1)S(1)} %copy.12, f32[1024]{0:T(1024)S(1)} %bitcast.32, bf16[8,10,16,1024]{3,2,1,0:T(8,128)(2,1)} %get-tuple-element.7, bf16[8,10,16,512]{3,2,1,0:T(8,128)(2,1)} %get-tuple-element.8), kind=kOutput, calls=%fused_computation.1 | convolution fusion | flops 1344273408 | bytes 7086080 | tf_op jit(solution)/shard_map/dot_general | solution.py:24
  141.3 1.8 %copy.9 = f32[1,1024,512]{2,1,0:T(8,128)} copy(f32[1,1024,512]{1,2,0:T(8,128)S(1)} %get-tuple-element.15) | data formatting | bytes 4194304
  143.1 5.0 %convolution_bitcast_fusion = f32[1,1024,512]{2,1,0:T(8,128)} fusion(bf16[8,10,16,1024]{3,2,1,0:T(8,128)(2,1)} %get-tuple-element.9, bf16[8,10,16,512]{3,2,1,0:T(8,128)(2,1)} %get-tuple-element.10), kind=kOutput, calls=%fused_computation.4 | convolution fusion | flops 1342177280 | bytes 6029312 | tf_op jit(solution)/shard_map/dot_general | solution.py:24
where the time goes:
time: 148 us
  Pallas kernels  134 us (91%)
  matrix products  9.27 us (6%)
  local copies, waits for them, and re-layouts  4.32 us (3%)
    pallas_call x1, Pallas kernels, local(): pl.pallas_call(functools.partial(relay_kernel, sections, replicas, micros...  134 us
    dot_general x2, matrix products, column_product(): lax.dot_general(left, right, (((0,), (0,)), ((), ())), preferred_element_...  9.27 us

commit v1 on v0

v1 whole, which is shorter than its diff:
```python
import functools

import jax
import jax.numpy as jnp
from jax import lax
from jax.experimental import pallas as pl
from jax.experimental.pallas import tpu as pltpu
from jax.sharding import PartitionSpec as P

ROWS = 16
WCHUNK = 1024
DELAY = 1
EPSILON = 1e-05
MESH = pl.DeviceIdType.MESH


def nt_dot(left, right):
    return lax.dot_general(
        left, right, (((1,), (1,)), ((), ())), preferred_element_type=jnp.float32
    )


def relay_kernel(
    sections,
    replicas,
    micros,
    x_ref,
    c_ref,
    win_hbm,
    wout_hbm,
    gain_ref,
    all_h,
    all_g,
    all_act,
    all_du,
    win,
    wout,
    win_t,
    wout_t,
    stash,
    up,
    out_f,
    out_b,
    act_buf,
    du_buf,
    pre,
    scale,
    w_sem,
    f_recv,
    b_recv,
    f_send,
    b_send,
    x_recv,
    x_send,
):
    width = stash.shape[2]
    hidden = win.shape[1]
    quarter = width // 4
    pieces = ((0, quarter), (quarter, 2 * quarter), (3 * quarter, quarter))
    groups = ((0, 2), (2, 3))
    wchunks = width // WCHUNK
    pos = lax.axis_index("section")
    block = width // replicas
    me = lax.axis_index("dp")
    is_first = pos == 0
    is_last = pos == sections - 1
    not_first = pos > 0
    not_last = pos < sections - 1

    def wcopy(kind, i):
        rows = pl.ds(pl.multiple_of(i * WCHUNK, WCHUNK), WCHUNK)
        src, dst = ((win_hbm, win), (wout_hbm, wout))[kind]
        return pltpu.make_async_copy(src.at[rows, :], dst.at[rows, :], w_sem.at[kind, i])

    def load_weights(kind):
        @pl.loop(0, wchunks)
        def _(i):
            wcopy(kind, i).start()

    @pl.when(is_first)
    def _():
        for m in range(micros):
            for k, (start, size) in enumerate(pieces):
                pltpu.make_async_copy(
                    x_ref.at[m, :, pl.ds(start, size)],
                    stash.at[m, :, pl.ds(start, size)],
                    f_recv.at[m, k],
                ).start()
            if m == 0:
                load_weights(0)
                load_weights(1)

    @pl.when(not_first)
    def _():
        load_weights(1)
        load_weights(0)

    @pl.when(is_last)
    def _():
        for m in range(micros):
            for k, (start, size) in enumerate(pieces):
                pltpu.make_async_copy(
                    c_ref.at[m, :, pl.ds(start, size)],
                    up.at[m, :, pl.ds(start, size)],
                    b_recv.at[m, k],
                ).start()

    barrier = pltpu.get_barrier_semaphore()

    @pl.when(not_first)
    def _():
        pl.semaphore_signal(
            barrier, inc=1, device_id={"section": pos - 1}, device_id_type=MESH
        )

    @pl.when(not_last)
    def _():
        pl.semaphore_signal(
            barrier, inc=1, device_id={"section": pos + 1}, device_id_type=MESH
        )

    @pl.loop(1, replicas)
    def _(step):
        pl.semaphore_signal(
            barrier,
            inc=1,
            device_id={"dp": lax.rem(me + step, replicas)},
            device_id_type=MESH,
        )

    pl.semaphore_wait(
        barrier,
        replicas - 1 + not_first.astype(jnp.int32) + not_last.astype(jnp.int32),
    )

    @pl.when(not_first)
    def _():
        @pl.loop(0, wchunks)
        def _(i):
            wcopy(1, i).wait()

            @pl.when(not_last)
            def _():
                rows = pl.ds(pl.multiple_of(i * WCHUNK, WCHUNK), WCHUNK)
                wout_t[:, rows] = wout[rows, :].T

        @pl.loop(0, wchunks)
        def _(i):
            rows = pl.ds(pl.multiple_of(i * WCHUNK, WCHUNK), WCHUNK)
            wcopy(0, i).wait()
            win_t[:, rows] = win[rows, :].T

    def send_forward(m, k):
        start, size = pieces[k]
        return pltpu.make_async_remote_copy(
            src_ref=out_f.at[m, :, pl.ds(start, size)],
            dst_ref=stash.at[m, :, pl.ds(start, size)],
            send_sem=f_send.at[m, k],
            recv_sem=f_recv.at[m, k],
            device_id={"section": pos + 1},
            device_id_type=MESH,
        )

    def send_backward(m, k):
        start, size = pieces[k]
        return pltpu.make_async_remote_copy(
            src_ref=out_b.at[m, :, pl.ds(start, size)],
            dst_ref=up.at[m, :, pl.ds(start, size)],
            send_sem=b_send.at[m, k],
            recv_sem=b_recv.at[m, k],
            device_id={"section": pos - 1},
            device_id_type=MESH,
        )

    def arrived(buffer, sems, m, k):
        start, size = pieces[k]
        piece = buffer.at[m, :, pl.ds(start, size)]
        pltpu.make_async_copy(piece, piece, sems.at[m, k]).wait()

    def span(first, past):
        start = pieces[first][0]
        return start, pieces[past - 1][0] + pieces[past - 1][1] - start

    def share(kind, src_of, dst):
        pltpu.make_async_copy(src_of(me), dst, x_recv.at[kind]).start()

        @pl.loop(1, replicas)
        def _(step):
            peer = lax.rem(me + step, replicas)
            pltpu.make_async_remote_copy(
                src_ref=src_of(peer),
                dst_ref=dst,
                send_sem=x_send.at[kind],
                recv_sem=x_recv.at[kind],
                device_id={"dp": peer},
                device_id_type=MESH,
            ).start()

    def part(owner):
        return pl.ds(pl.multiple_of(owner * block, block), block)

    def forward(m):
        total = jnp.zeros((ROWS, 1), jnp.float32)
        u = jnp.zeros((ROWS, hidden), jnp.float32)
        for first, past in groups:
            start, size = span(first, past)
            for k in range(first, past):
                arrived(stash, f_recv, m, k)

            @pl.when((m == 0) & is_first)
            def _():
                @pl.loop(start // WCHUNK, (start + size) // WCHUNK)
                def _(i):
                    wcopy(0, i).wait()

            h = stash[m, :, start : start + size].astype(jnp.float32)
            scaled = (h * gain_ref[:, start : start + size]).astype(jnp.bfloat16)
            total = total + jnp.sum(h * h, axis=1, keepdims=True)
            u = u + jnp.dot(
                scaled, win[start : start + size, :], preferred_element_type=jnp.float32
            )
        inv = lax.rsqrt(total / width + EPSILON)
        u = u * inv
        act = (u * jax.nn.sigmoid(u)).astype(jnp.bfloat16)
        pre[m] = u
        scale[m] = jnp.broadcast_to(inv, scale.shape[1:])
        act_buf[m] = act

        @pl.when((m == 0) & is_first)
        def _():
            @pl.loop(0, wchunks)
            def _(i):
                wcopy(1, i).wait()

        def emit(product):
            for k, (start, size) in enumerate(pieces):
                cols = slice(start, start + size)
                h = stash[m, :, cols].astype(jnp.float32)
                out_f[m, :, cols] = (h + product(cols)).astype(jnp.bfloat16)
                send_forward(m, k).start()

        @pl.when(is_first)
        def _():
            emit(lambda cols: nt_dot(act, wout[cols, :]))

        @pl.when(not_first & not_last)
        def _():
            emit(
                lambda cols: jnp.dot(
                    act, wout_t[:, cols], preferred_element_type=jnp.float32
                )
            )

        share(0, lambda owner: stash.at[m, :, part(owner)], all_h.at[me, m])
        share(1, lambda owner: act_buf.at[m], all_act.at[me, m])

    def backward(m):
        da = jnp.zeros((ROWS, hidden), jnp.float32)
        for first, past in groups:
            start, size = span(first, past)
            for k in range(first, past):
                arrived(up, b_recv, m, k)
            da = da + jnp.dot(
                up[m, :, start : start + size],
                wout[start : start + size, :],
                preferred_element_type=jnp.float32,
            )
        u = pre[m]
        inv = scale[m][:, :1]
        sig = jax.nn.sigmoid(u)
        wide_du = da * sig * (1.0 + u * (1.0 - sig))
        du = wide_du.astype(jnp.bfloat16)
        du_buf[m] = (wide_du * inv).astype(jnp.bfloat16)
        centered = jnp.sum(du.astype(jnp.float32) * u, axis=1, keepdims=True) / (
            inv * width
        )
        pull = inv * inv * inv * centered

        @pl.when(not_first)
        def _():
            for k, (start, size) in enumerate(pieces):
                cols = slice(start, start + size)
                h = stash[m, :, cols].astype(jnp.float32)
                g = up[m, :, cols].astype(jnp.float32)
                dn = jnp.dot(du, win_t[:, cols], preferred_element_type=jnp.float32)
                out_b[m, :, cols] = (
                    g + inv * (dn * gain_ref[:, cols]) - h * pull
                ).astype(jnp.bfloat16)
                send_backward(m, k).start()

        share(2, lambda owner: up.at[m, :, part(owner)], all_g.at[me, m])
        share(3, lambda owner: du_buf.at[m], all_du.at[me, m])

    @pl.loop(0, micros + 2 * DELAY * (sections - 1))
    def _(tick):
        mf = tick - DELAY * pos
        mb = tick - DELAY * (2 * (sections - 1) - pos)

        @pl.when((mf >= 0) & (mf < micros))
        def _():
            forward(mf)

        @pl.when((mb >= 0) & (mb < micros))
        def _():
            backward(mb)

    @pl.loop(0, micros)
    def _(m):
        for k in range(len(pieces)):

            @pl.when(not_last)
            def _():
                send_forward(m, k).wait_send()

            @pl.when(not_first)
            def _():
                send_backward(m, k).wait_send()

    for kind, ref in enumerate((all_h, all_act, all_g, all_du)):
        sent = ref.at[pl.ds(0, replicas - 1)]
        pltpu.make_async_copy(sent, sent, x_send.at[kind]).wait()
        pltpu.make_async_copy(ref, ref, x_recv.at[kind]).wait()


def grad_kernel(me_ref, h_ref, g_ref, act_ref, du_ref, win_ref, gain_ref, din, dout, dgain):
    raw = jnp.dot(h_ref[...].T, du_ref[...], preferred_element_type=jnp.float32)
    rows = raw.shape[0]
    gain = jnp.broadcast_to(gain_ref[...], (128, rows)).T[:, :1]
    din[...] = raw * gain
    sums = jnp.sum(win_ref[...].astype(jnp.float32) * raw, axis=1, keepdims=True)
    dgain[...] = jnp.broadcast_to(sums, (rows, 128)).T[:1]
    dout[...] = jnp.dot(g_ref[...].T, act_ref[...], preferred_element_type=jnp.float32)


def gradients(me, h, g, act, du, weight_in, gains):
    total, block = h.shape
    hidden = act.shape[1]
    rows = min(256, block)
    steps = block // rows
    tall = pl.BlockSpec((total, rows), lambda i, me_ref: (0, i))
    whole = pl.BlockSpec((total, hidden), lambda i, me_ref: (0, 0))
    out = pl.BlockSpec((rows, hidden), lambda i, me_ref: (i, 0))
    return pl.pallas_call(
        grad_kernel,
        grid_spec=pltpu.PrefetchScalarGridSpec(
            num_scalar_prefetch=1,
            grid=(steps,),
            in_specs=[
                tall,
                tall,
                whole,
                whole,
                pl.BlockSpec((rows, hidden), lambda i, me_ref: (me_ref[0] * steps + i, 0)),
                pl.BlockSpec((1, rows), lambda i, me_ref: (0, me_ref[0] * steps + i)),
            ],
            out_specs=[out, out, pl.BlockSpec((1, rows), lambda i, me_ref: (0, i))],
        ),
        out_shape=(
            jax.ShapeDtypeStruct((block, hidden), jnp.float32),
            jax.ShapeDtypeStruct((block, hidden), jnp.float32),
            jax.ShapeDtypeStruct((1, block), jnp.float32),
        ),
        compiler_params=pltpu.CompilerParams(vmem_limit_bytes=32 * 2**20),
    )(me, h, g, act, du, weight_in, gains)


def local(sections, replicas, inputs, cotangent, weight_in, weight_out, norm_gains):
    tokens, width = inputs.shape
    hidden = weight_in.shape[2]
    micros = tokens // ROWS
    block = width // replicas
    wide = jax.ShapeDtypeStruct((replicas, micros, ROWS, block), jnp.bfloat16)
    narrow = jax.ShapeDtypeStruct((replicas, micros, ROWS, hidden), jnp.bfloat16)
    any_spec = pl.BlockSpec(memory_space=pl.ANY)
    vmem_spec = pl.BlockSpec(memory_space=pltpu.VMEM)
    wide_scratch = pltpu.VMEM((micros, ROWS, width), jnp.bfloat16)
    weight_scratch = pltpu.VMEM((width, hidden), jnp.bfloat16)
    flipped_scratch = pltpu.VMEM((hidden, width), jnp.bfloat16)
    dma = pltpu.SemaphoreType.DMA
    all_h, all_g, all_act, all_du = pl.pallas_call(
        functools.partial(relay_kernel, sections, replicas, micros),
        out_shape=(wide, wide, narrow, narrow),
        in_specs=[any_spec] * 4 + [vmem_spec],
        out_specs=(any_spec,) * 4,
        scratch_shapes=[
            weight_scratch,
            weight_scratch,
            flipped_scratch,
            flipped_scratch,
            wide_scratch,
            wide_scratch,
            wide_scratch,
            wide_scratch,
            pltpu.VMEM((micros, ROWS, hidden), jnp.bfloat16),
            pltpu.VMEM((micros, ROWS, hidden), jnp.bfloat16),
            pltpu.VMEM((micros, ROWS, hidden), jnp.float32),
            pltpu.VMEM((micros, ROWS, 128), jnp.float32),
            dma((2, width // WCHUNK)),
            dma((micros, 3)),
            dma((micros, 3)),
            dma((micros, 3)),
            dma((micros, 3)),
            dma((4,)),
            dma((4,)),
        ],
        compiler_params=pltpu.CompilerParams(
            collective_id=0, has_side_effects=True, vmem_limit_bytes=62 * 2**20
        ),
    )(
        inputs.reshape(micros, ROWS, width),
        cotangent.reshape(micros, ROWS, width),
        weight_in[0],
        weight_out[0],
        norm_gains,
    )
    total = replicas * tokens
    me = lax.axis_index("dp").astype(jnp.int32).reshape(1)
    in_grad, out_grad, gain_grad = gradients(
        me,
        all_h.reshape(total, block),
        all_g.reshape(total, block),
        all_act.reshape(total, hidden),
        all_du.reshape(total, hidden),
        weight_in[0],
        norm_gains,
    )
    return (in_grad[None], out_grad[None], gain_grad)


def solution(mesh):
    return jax.shard_map(
        functools.partial(local, mesh.shape["section"], mesh.shape["dp"]),
        mesh=mesh,
        in_specs=(
            P("dp", None),
            P("dp", None),
            P("section", None, None),
            P("section", None, None),
            P("section", None),
        ),
        out_specs=(P("section", "dp", None), P("section", "dp", None), P("section", "dp")),
        check_vma=False,
    )
```

time: 148 us -> 149 us (level)
  matrix products: 9.27 us -> 0 us
  local copies, waits for them, and re-layouts: 4.32 us -> 9.49 us
  Pallas kernels: 134 us -> 138 us
    dot_general x2 -> x0, matrix products: 9.27 us -> none  [column_product(): lax.dot_general(left, right, (((0,), (0,)), ((), ())), preferred_element_...]
    unnamed x2 -> x12, local copies, waits for them, and re-layouts: 2.34 us -> 9.49 us
    pallas_call x0 -> x1, Pallas kernels: none -> 5.08 us  [gradients(): pl.pallas_call(grad_kernel, grid_spec=pltpu.PrefetchScalarGridSpec(num_sc...]
    dynamic_slice x2 -> x0, local copies, waits for them, and re-layouts: 1.98 us -> none  [the longest x1 1.29 us: local(): own_rows = lax.dynamic_slice_in_dim(weight_in[0], own, block, 0)]
where the time goes in v1:
time: 149 us; the launch traced here: 148 us
  Pallas kernels  138 us (93%)
  local copies, waits for them, and re-layouts  9.49 us (6%)
    pallas_call x1, Pallas kernels, local(): pl.pallas_call(functools.partial(relay_kernel, sections, replicas, micros...  133 us
    unnamed x12, local copies, waits for them, and re-layouts  9.49 us
    pallas_call x1, Pallas kernels, gradients(): pl.pallas_call(grad_kernel, grid_spec=pltpu.PrefetchScalarGridSpec(num_sc...  5.08 us

profile of v1, /device:TPU:0, one launch (start us, length us, event | category | flops | bytes accessed | tf_op | source)
XLA Modules:
  0.0 148.2 jit_solution(1436380274559405527)
XLA Ops:
  0.6 0.0 copy-start.5
  0.6 132.9 %shard_map.76 = (bf16[8,10,16,1024]{3,2,1,0:T(8,128)(2,1)}, bf16[8,10,16,1024]{3,2,1,0:T(8,128)(2,1)}, bf16[8,10,16,512]{3,2,1,0:T(8,128)(2,1)}, bf16[8,10,16,512]{3,2,1,0:T(8,128)(2,1)}) custom-call(bf16[10,16,8192]{2,1,0:T(8,128)(2,1)} %bitcast.18, bf16[10,16,8192]{2,1,0:T(8,128)(2,1)} %bitcast.19, bf16[8192,512]{1,0:T(8,128)(2,1)} %bitcast.11, ...), custom_call_target="tpu_custom_call" | custom-call | tf_op jit(solution)/shard_map/pallas_call | solution.py:380
  133.6 0.0 copy-done.5
  133.6 0.0 copy-start
  133.6 3.4 %copy-done = bf16[1,8192,512]{2,1,0:T(8,128)(2,1)S(1)} copy-done((bf16[1,8192,512]{2,1,0:T(8,128)(2,1)S(1)}, bf16[1,8192,512]{2,1,0:T(8,128)(2,1)}, u32[]{:S(2)}) %copy-start) | copy-done | bytes 8388632
  137.0 0.0 copy-start.1
  137.0 1.7 %copy-done.1 = bf16[8,10,16,1024]{3,2,1,0:T(8,128)(2,1)S(1)} copy-done((bf16[8,10,16,1024]{3,2,1,0:T(8,128)(2,1)S(1)}, bf16[8,10,16,1024]{3,2,1,0:T(8,128)(2,1)}, u32[]{:S(2)}) %copy-start.1) | copy-done | bytes 2621464
  138.7 0.0 copy-start.2
  138.7 1.7 %copy-done.2 = bf16[8,10,16,1024]{3,2,1,0:T(8,128)(2,1)S(1)} copy-done((bf16[8,10,16,1024]{3,2,1,0:T(8,128)(2,1)S(1)}, bf16[8,10,16,1024]{3,2,1,0:T(8,128)(2,1)}, u32[]{:S(2)}) %copy-start.2) | copy-done | bytes 2621464
  140.4 0.0 copy-start.3
  140.4 1.3 copy-done.3
  141.8 0.0 copy-start.4
  141.8 1.3 copy-done.4
  143.1 5.1 %shard_map.77 = (f32[1024,512]{1,0:T(8,128)}, f32[1024,512]{1,0:T(8,128)}, f32[1,1024]{1,0:T(1,128)}) custom-call(s32[1]{0:T(128)} %bitcast.me_ref, bf16[1280,1024]{1,0:T(8,128)(2,1)S(1)} %bitcast.13, bf16[1280,1024]{1,0:T(8,128)(2,1)S(1)} %bitcast.14, bf16[1280,512]{1,0:T(8,128)(2,1)S(1)} %bitcast.15, bf16[1280,512]{1,0:T(8,128)(2,1)S(1)} %bitcast.16, ...), custom_call_target="tpu_custom_call" | custom-call | tf_op jit(solution)/shard_map/pallas_call | solution.py:343
Async XLA Ops:
  0.6 132.9 %copy-start.5 = (f32[1,8192]{1,0:T(1,128)S(1)}, f32[1,8192]{1,0:T(1,128)}, u32[]{:S(2)}) copy-start(f32[1,8192]{1,0:T(1,128)} %gain_ref.3) | copy-start | bytes 98308
  133.6 3.4 %copy-start = (bf16[1,8192,512]{2,1,0:T(8,128)(2,1)S(1)}, bf16[1,8192,512]{2,1,0:T(8,128)(2,1)}, u32[]{:S(2)}) copy-start(bf16[1,8192,512]{2,1,0:T(8,128)(2,1)} %param.7) | copy-start | bytes 25165828
  137.0 1.7 %copy-start.1 = (bf16[8,10,16,1024]{3,2,1,0:T(8,128)(2,1)S(1)}, bf16[8,10,16,1024]{3,2,1,0:T(8,128)(2,1)}, u32[]{:S(2)}) copy-start(bf16[8,10,16,1024]{3,2,1,0:T(8,128)(2,1)} %get-tuple-element.10) | copy-start | bytes 7864324
  138.7 1.7 %copy-start.2 = (bf16[8,10,16,1024]{3,2,1,0:T(8,128)(2,1)S(1)}, bf16[8,10,16,1024]{3,2,1,0:T(8,128)(2,1)}, u32[]{:S(2)}) copy-start(bf16[8,10,16,1024]{3,2,1,0:T(8,128)(2,1)} %get-tuple-element.11) | copy-start | bytes 7864324
  140.4 1.3 copy-start.3
  141.8 1.3 copy-start.4

commit v2 on v1

v2 whole, which is shorter than its diff:
```python
import functools

import jax
import jax.numpy as jnp
from jax import lax
from jax.experimental import pallas as pl
from jax.experimental.pallas import tpu as pltpu
from jax.sharding import PartitionSpec as P

ROWS = 16
LAG = 10
EPSILON = 1e-05
MESH = pl.DeviceIdType.MESH


def dot(left, right):
    return jnp.dot(left, right, preferred_element_type=jnp.float32)


def nt_dot(left, right):
    return lax.dot_general(
        left, right, (((1,), (1,)), ((), ())), preferred_element_type=jnp.float32
    )


def relay_kernel(
    sections,
    replicas,
    micros,
    x_ref,
    c_ref,
    win_hbm,
    wout_hbm,
    gain_ref,
    all_h,
    all_g,
    all_act,
    all_du,
    win,
    wout,
    win_t,
    wout_t,
    gain,
    stash,
    up,
    out_f,
    out_b,
    act_buf,
    du_buf,
    pre,
    scale,
    fx_send,
    fx_recv,
    bx_send,
    bx_recv,
    w_sem,
    f_recv,
    b_recv,
    f_send,
    b_send,
    fx_sem,
    bx_sem,
    xs_sem,
    x_recv,
    x_send,
):
    half = stash.shape[2]
    width = 2 * half
    hidden = win.shape[1]
    count = 2 * micros
    block = width // replicas
    chips = replicas // 2
    quarter = half // 4
    pieces = ((0, quarter), (quarter, 2 * quarter), (3 * quarter, quarter))
    take = ((0, 3),)
    give = ((0, 3),)
    piece_of = [
        [k for k, (start, size) in enumerate(pieces) if start <= j * block < start + size][0]
        for j in range(chips)
    ]
    pos = lax.axis_index("section")
    me = lax.axis_index("dp")
    chip = me // 2
    core = lax.rem(me, 2)
    partner = me + 1 - 2 * core
    is_first = pos == 0
    is_last = pos == sections - 1
    not_first = pos > 0
    not_last = pos < sections - 1

    def part(owner):
        return pl.ds(pl.multiple_of(owner * block, block), block)

    def mine(j):
        return slice(j * block, (j + 1) * block)

    def span(first, past):
        start = pieces[first][0]
        return start, pieces[past - 1][0] + pieces[past - 1][1]

    def wcopy(kind, j):
        src, dst = ((win_hbm, win), (wout_hbm, wout))[kind]
        return pltpu.make_async_copy(
            src.at[part(2 * j + core), :], dst.at[mine(j), :], w_sem.at[kind, j]
        )

    def load_weights(kind):
        for j in range(chips):
            wcopy(kind, j).start()

    def load_own(src, dst, sems, m):
        for j in range(chips):
            pltpu.make_async_copy(
                src.at[m, :, part(2 * j + core)],
                dst.at[2 * m + core, :, mine(j)],
                sems.at[2 * m + core, piece_of[j]],
            ).start()

    def push_partner(src, dst, sems, m):
        for j in range(chips):
            pltpu.make_async_remote_copy(
                src_ref=src.at[m, :, part(2 * j + 1 - core)],
                dst_ref=dst.at[2 * m + core, :, mine(j)],
                send_sem=xs_sem.at[0],
                recv_sem=sems.at[2 * m + core, piece_of[j]],
                device_id={"dp": partner},
                device_id_type=MESH,
            ).start()

    def spread(src, dst, kind):
        @pl.loop(1, replicas)
        def _(step):
            peer = lax.rem(me + step, replicas)
            pltpu.make_async_remote_copy(
                src_ref=src.at[:, :, part(peer)],
                dst_ref=dst.at[me],
                send_sem=x_send.at[kind],
                recv_sem=x_recv.at[kind],
                device_id={"dp": peer},
                device_id_type=MESH,
            ).start()

    @pl.when(is_first)
    def _():
        load_own(x_ref, stash, f_recv, 0)
        load_weights(0)
        load_weights(1)

        @pl.loop(1, micros)
        def _(m):
            load_own(x_ref, stash, f_recv, m)

    @pl.when(not_first)
    def _():
        load_weights(1)
        load_weights(0)

    @pl.when(is_last)
    def _():
        @pl.loop(0, micros)
        def _(m):
            load_own(c_ref, up, b_recv, m)

    barrier = pltpu.get_barrier_semaphore()

    @pl.when(not_first)
    def _():
        pl.semaphore_signal(
            barrier, inc=1, device_id={"section": pos - 1}, device_id_type=MESH
        )

    @pl.when(not_last)
    def _():
        pl.semaphore_signal(
            barrier, inc=1, device_id={"section": pos + 1}, device_id_type=MESH
        )

    @pl.loop(1, replicas)
    def _(step):
        pl.semaphore_signal(
            barrier,
            inc=1,
            device_id={"dp": lax.rem(me + step, replicas)},
            device_id_type=MESH,
        )

    for j in range(chips):
        gain[:, mine(j)] = gain_ref[:, part(2 * j + core)]

    pl.semaphore_wait(
        barrier,
        replicas - 1 + not_first.astype(jnp.int32) + not_last.astype(jnp.int32),
    )

    @pl.when(is_first)
    def _():
        @pl.loop(0, micros)
        def _(m):
            push_partner(x_ref, stash, f_recv, m)

        spread(x_ref, all_h, 0)

    @pl.when(is_last)
    def _():
        @pl.loop(0, micros)
        def _(m):
            push_partner(c_ref, up, b_recv, m)

        spread(c_ref, all_g, 2)

    @pl.when(not_first)
    def _():
        for j in range(chips):
            wcopy(1, j).wait()

            @pl.when(not_last)
            def _():
                wout_t[:, mine(j)] = wout[mine(j), :].T

        for j in range(chips):
            wcopy(0, j).wait()
            win_t[:, mine(j)] = win[mine(j), :].T

    def send_forward(i, k):
        start, size = pieces[k]
        return pltpu.make_async_remote_copy(
            src_ref=out_f.at[i, :, pl.ds(start, size)],
            dst_ref=stash.at[i, :, pl.ds(start, size)],
            send_sem=f_send.at[i, k],
            recv_sem=f_recv.at[i, k],
            device_id={"section": pos + 1},
            device_id_type=MESH,
        )

    def send_backward(i, k):
        start, size = pieces[k]
        return pltpu.make_async_remote_copy(
            src_ref=out_b.at[i, :, pl.ds(start, size)],
            dst_ref=up.at[i, :, pl.ds(start, size)],
            send_sem=b_send.at[i, k],
            recv_sem=b_recv.at[i, k],
            device_id={"section": pos - 1},
            device_id_type=MESH,
        )

    def trade_forward(i):
        return pltpu.make_async_remote_copy(
            src_ref=fx_send.at[i],
            dst_ref=fx_recv.at[i],
            send_sem=xs_sem.at[1],
            recv_sem=fx_sem.at[i],
            device_id={"dp": partner},
            device_id_type=MESH,
        )

    def trade_backward(i):
        return pltpu.make_async_remote_copy(
            src_ref=bx_send.at[i],
            dst_ref=bx_recv.at[i],
            send_sem=xs_sem.at[2],
            recv_sem=bx_sem.at[i],
            device_id={"dp": partner},
            device_id_type=MESH,
        )

    def arrived(buffer, sems, i, first, past):
        for k in range(first, past):
            start, size = pieces[k]
            piece = buffer.at[i, :, pl.ds(start, size)]
            pltpu.make_async_copy(piece, piece, sems.at[i, k]).wait()

    def share(kind, i, src_of, dst):
        slot = dst.at[2 * chip + lax.rem(i, 2), i // 2]
        pltpu.make_async_copy(src_of(chip), slot, x_recv.at[kind]).start()
        for step in range(1, chips):
            target = lax.rem(chip + step, chips)
            pltpu.make_async_remote_copy(
                src_ref=src_of(target),
                dst_ref=slot,
                send_sem=x_send.at[kind],
                recv_sem=x_recv.at[kind],
                device_id={"dp": 2 * target + core},
                device_id_type=MESH,
            ).start()

    def keep_own(kind, i, src, dst):
        @pl.when(lax.rem(i, 2) == core)
        def _():
            pltpu.make_async_copy(
                src.at[i, :, part(chip)], dst.at[me, i // 2], x_recv.at[kind]
            ).start()

    def forward_in(i):
        total = jnp.zeros((ROWS, 1), jnp.float32)
        u = jnp.zeros((ROWS, hidden), jnp.float32)
        for first, past in take:
            start, stop = span(first, past)
            arrived(stash, f_recv, i, first, past)

            @pl.when((i == 0) & is_first)
            def _():
                for j in range(chips):
                    if start <= j * block < stop:
                        wcopy(0, j).wait()

            h = stash[i, :, start:stop].astype(jnp.float32)
            scaled = (h * gain[:, start:stop]).astype(jnp.bfloat16)
            total = total + jnp.sum(h * h, axis=1, keepdims=True)
            u = u + dot(scaled, win[start:stop, :])
        fx_send[i, :, :hidden] = u
        fx_send[i, :, hidden:] = jnp.broadcast_to(total, (ROWS, 128))
        trade_forward(i).start()

        @pl.when(is_first)
        def _():
            keep_own(0, i, stash, all_h)

        @pl.when(not_first)
        def _():
            share(0, i, lambda j: stash.at[i, :, part(j)], all_h)

    def forward_out(i):
        pltpu.make_async_copy(fx_recv.at[i], fx_recv.at[i], fx_sem.at[i]).wait()
        total = fx_send[i, :, hidden:] + fx_recv[i, :, hidden:]
        inv = lax.rsqrt(total / width + EPSILON)
        scale[i] = inv
        u = (fx_send[i, :, :hidden] + fx_recv[i, :, :hidden]) * inv[:, :1]
        act = (u * jax.nn.sigmoid(u)).astype(jnp.bfloat16)
        pre[i] = u
        act_buf[i] = act

        @pl.when((i == 0) & is_first)
        def _():
            for j in range(chips):
                wcopy(1, j).wait()

        def emit(product):
            for first, past in give:
                start, stop = span(first, past)
                h = stash[i, :, start:stop].astype(jnp.float32)
                out_f[i, :, start:stop] = (h + product(act, start, stop)).astype(
                    jnp.bfloat16
                )
                for k in range(first, past):
                    send_forward(i, k).start()

        @pl.when(is_first)
        def _():
            emit(lambda a, start, stop: nt_dot(a, wout[start:stop, :]))

        @pl.when(not_first & not_last)
        def _():
            emit(lambda a, start, stop: dot(a, wout_t[:, start:stop]))

        share(1, i, lambda j: act_buf.at[i], all_act)

    def backward_in(i):
        da = jnp.zeros((ROWS, hidden), jnp.float32)
        for first, past in take:
            start, stop = span(first, past)
            arrived(up, b_recv, i, first, past)
            da = da + dot(up[i, :, start:stop], wout[start:stop, :])
        bx_send[i] = da
        trade_backward(i).start()

        @pl.when(is_last)
        def _():
            keep_own(2, i, up, all_g)

        @pl.when(not_last)
        def _():
            share(2, i, lambda j: up.at[i, :, part(j)], all_g)

    def backward_out(i):
        pltpu.make_async_copy(bx_recv.at[i], bx_recv.at[i], bx_sem.at[i]).wait()
        da = bx_send[i] + bx_recv[i]
        u = pre[i]
        inv = scale[i][:, :1]
        sig = jax.nn.sigmoid(u)
        wide_du = da * sig * (1.0 + u * (1.0 - sig))
        du = wide_du.astype(jnp.bfloat16)
        du_buf[i] = (wide_du * inv).astype(jnp.bfloat16)

        @pl.when(not_first)
        def _():
            centered = jnp.sum(du.astype(jnp.float32) * u, axis=1, keepdims=True) / (
                inv * width
            )
            pull = inv * inv * inv * centered
            for first, past in give:
                start, stop = span(first, past)
                h = stash[i, :, start:stop].astype(jnp.float32)
                g = up[i, :, start:stop].astype(jnp.float32)
                dn = dot(du, win_t[:, start:stop])
                out_b[i, :, start:stop] = (
                    g + inv * (dn * gain[:, start:stop]) - h * pull
                ).astype(jnp.bfloat16)
                for k in range(first, past):
                    send_backward(i, k).start()

        share(3, i, lambda j: du_buf.at[i], all_du)

    lag = jnp.minimum(LAG * (sections - 1 - pos) // 2, count)
    lead = is_first.astype(jnp.int32)

    @pl.loop(0, count + lag + lead)
    def _(step):
        ahead = step - lead
        back = step - lag

        @pl.when(step < count)
        def _():
            forward_in(step)

        @pl.when((back >= 0) & (back < count))
        def _():
            backward_in(back)

        @pl.when((ahead >= 0) & (ahead < count))
        def _():
            forward_out(ahead)

        @pl.when((back >= 0) & (back < count))
        def _():
            backward_out(back)

    @pl.loop(0, count)
    def _(i):
        for k in range(len(pieces)):

            @pl.when(not_last)
            def _():
                send_forward(i, k).wait_send()

            @pl.when(not_first)
            def _():
                send_backward(i, k).wait_send()

    def drain(ref, sem):
        pltpu.make_async_copy(ref, ref, sem).wait()

    @pl.when(is_first | is_last)
    def _():
        drain(stash.at[pl.ds(0, micros)], xs_sem.at[0])

    drain(fx_send, xs_sem.at[1])
    drain(bx_send, xs_sem.at[2])
    for kind, ref, early in (
        (0, all_h, is_first),
        (1, all_act, False),
        (2, all_g, is_last),
        (3, all_du, False),
    ):
        drain(ref.at[pl.ds(0, replicas - 2)], x_send.at[kind])
        if early is not False:

            @pl.when(early)
            def _():
                drain(ref.at[0], x_send.at[kind])

        drain(ref, x_recv.at[kind])


def grad_kernel(me_ref, h_ref, g_ref, act_ref, du_ref, win_ref, gain_ref, din, dout, dgain):
    raw = jnp.dot(h_ref[...].T, du_ref[...], preferred_element_type=jnp.float32)
    rows = raw.shape[0]
    gain = jnp.broadcast_to(gain_ref[...], (128, rows)).T[:, :1]
    din[...] = raw * gain
    sums = jnp.sum(win_ref[...].astype(jnp.float32) * raw, axis=1, keepdims=True)
    dgain[...] = jnp.broadcast_to(sums, (rows, 128)).T[:1]
    dout[...] = jnp.dot(g_ref[...].T, act_ref[...], preferred_element_type=jnp.float32)


def gradients(me, h, g, act, du, weight_in, gains):
    total, block = h.shape
    hidden = act.shape[1]
    rows = min(256, block)
    steps = block // rows
    tall = pl.BlockSpec((total, rows), lambda i, me_ref: (0, i))
    whole = pl.BlockSpec((total, hidden), lambda i, me_ref: (0, 0))
    out = pl.BlockSpec((rows, hidden), lambda i, me_ref: (i, 0))
    return pl.pallas_call(
        grad_kernel,
        grid_spec=pltpu.PrefetchScalarGridSpec(
            num_scalar_prefetch=1,
            grid=(steps,),
            in_specs=[
                tall,
                tall,
                whole,
                whole,
                pl.BlockSpec((rows, hidden), lambda i, me_ref: (me_ref[0] * steps + i, 0)),
                pl.BlockSpec((1, rows), lambda i, me_ref: (0, me_ref[0] * steps + i)),
            ],
            out_specs=[out, out, pl.BlockSpec((1, rows), lambda i, me_ref: (0, i))],
        ),
        out_shape=(
            jax.ShapeDtypeStruct((block, hidden), jnp.float32),
            jax.ShapeDtypeStruct((block, hidden), jnp.float32),
            jax.ShapeDtypeStruct((1, block), jnp.float32),
        ),
        compiler_params=pltpu.CompilerParams(vmem_limit_bytes=62 * 2**20),
    )(me, h, g, act, du, weight_in, gains)


def local(sections, replicas, inputs, cotangent, weight_in, weight_out, norm_gains):
    tokens, width = inputs.shape
    hidden = weight_in.shape[2]
    micros = tokens // ROWS
    count = 2 * micros
    block = width // replicas
    half = width // 2
    wide = jax.ShapeDtypeStruct((replicas, micros, ROWS, block), jnp.bfloat16)
    narrow = jax.ShapeDtypeStruct((replicas, micros, ROWS, hidden), jnp.bfloat16)
    any_spec = pl.BlockSpec(memory_space=pl.ANY)
    vmem_spec = pl.BlockSpec(memory_space=pltpu.VMEM)
    wide_scratch = pltpu.VMEM((count, ROWS, half), jnp.bfloat16)
    narrow_scratch = pltpu.VMEM((count, ROWS, hidden), jnp.bfloat16)
    sums_scratch = pltpu.VMEM((count, ROWS, hidden + 128), jnp.float32)
    rows_scratch = pltpu.VMEM((count, ROWS, hidden), jnp.float32)
    dma = pltpu.SemaphoreType.DMA
    all_h, all_g, all_act, all_du = pl.pallas_call(
        functools.partial(relay_kernel, sections, replicas, micros),
        out_shape=(wide, wide, narrow, narrow),
        in_specs=[any_spec] * 4 + [vmem_spec],
        out_specs=(any_spec,) * 4,
        scratch_shapes=[
            pltpu.VMEM((half, hidden), jnp.bfloat16),
            pltpu.VMEM((half, hidden), jnp.bfloat16),
            pltpu.VMEM((hidden, half), jnp.bfloat16),
            pltpu.VMEM((hidden, half), jnp.bfloat16),
            pltpu.VMEM((1, half), jnp.float32),
            wide_scratch,
            wide_scratch,
            wide_scratch,
            wide_scratch,
            narrow_scratch,
            narrow_scratch,
            rows_scratch,
            pltpu.VMEM((count, ROWS, 128), jnp.float32),
            sums_scratch,
            sums_scratch,
            rows_scratch,
            rows_scratch,
            dma((2, replicas // 2)),
            dma((count, 3)),
            dma((count, 3)),
            dma((count, 3)),
            dma((count, 3)),
            dma((count,)),
            dma((count,)),
            dma((3,)),
            dma((4,)),
            dma((4,)),
        ],
        compiler_params=pltpu.CompilerParams(
            collective_id=0, has_side_effects=True, vmem_limit_bytes=62 * 2**20
        ),
    )(
        inputs.reshape(micros, ROWS, width),
        cotangent.reshape(micros, ROWS, width),
        weight_in[0],
        weight_out[0],
        norm_gains,
    )
    total = replicas * tokens
    me = lax.axis_index("dp").astype(jnp.int32).reshape(1)
    in_grad, out_grad, gain_grad = gradients(
        me,
        all_h.reshape(total, block),
        all_g.reshape(total, block),
        all_act.reshape(total, hidden),
        all_du.reshape(total, hidden),
        weight_in[0],
        norm_gains,
    )
    return (in_grad[None], out_grad[None], gain_grad)


def solution(mesh):
    return jax.shard_map(
        functools.partial(local, mesh.shape["section"], mesh.shape["dp"]),
        mesh=mesh,
        in_specs=(
            P("dp", None),
            P("dp", None),
            P("section", None, None),
            P("section", None, None),
            P("section", None),
        ),
        out_specs=(P("section", "dp", None), P("section", "dp", None), P("section", "dp")),
        check_vma=False,
    )
```

time: 149 us -> 128 us (0.86)
  Pallas kernels: 138 us -> 128 us
  local copies, waits for them, and re-layouts: 9.49 us -> 0 us
    pallas_call x1, Pallas kernels: 133 us -> 120 us  [local(): pl.pallas_call(functools.partial(relay_kernel, sections, replicas, micros...]
    unnamed x12 -> x0, local copies, waits for them, and re-layouts: 9.49 us -> none
    pallas_call x1, Pallas kernels: 5.08 us -> 7.72 us  [gradients(): pl.pallas_call(grad_kernel, grid_spec=pltpu.PrefetchScalarGridSpec(num_sc...]
where the time goes in v2:
time: 128 us
  Pallas kernels  128 us (100%)
    pallas_call x1, Pallas kernels, local(): pl.pallas_call(functools.partial(relay_kernel, sections, replicas, micros...  120 us
    pallas_call x1, Pallas kernels, gradients(): pl.pallas_call(grad_kernel, grid_spec=pltpu.PrefetchScalarGridSpec(num_sc...  7.72 us

profile of v2, /device:TPU:0, one launch (start us, length us, event | category | flops | bytes accessed | tf_op | source)
XLA Modules:
  0.0 128.2 jit_solution(17914536649748471263)
XLA Ops:
  0.6 119.8 %shard_map.76 = (bf16[8,10,16,1024]{3,2,1,0:T(8,128)(2,1)}, bf16[8,10,16,1024]{3,2,1,0:T(8,128)(2,1)}, bf16[8,10,16,512]{3,2,1,0:T(8,128)(2,1)}, bf16[8,10,16,512]{3,2,1,0:T(8,128)(2,1)}) custom-call(bf16[10,16,8192]{2,1,0:T(8,128)(2,1)} %bitcast.16, bf16[10,16,8192]{2,1,0:T(8,128)(2,1)} %bitcast.17, bf16[8192,512]{1,0:T(8,128)(2,1)} %bitcast.11, ...), custom_call_target="tpu_custom_call" | custom-call | tf_op jit(solution)/shard_map/pallas_call | solution.py:522
  120.4 7.7 %shard_map.77 = (f32[1024,512]{1,0:T(8,128)}, f32[1024,512]{1,0:T(8,128)}, f32[1,1024]{1,0:T(1,128)}) custom-call(s32[1]{0:T(128)} %bitcast.me_ref, bf16[1280,1024]{1,0:T(8,128)(2,1)} %bitcast.14, bf16[1280,1024]{1,0:T(8,128)(2,1)} %bitcast.15, bf16[1280,512]{1,0:T(8,128)(2,1)} %bitcast.18, bf16[1280,512]{1,0:T(8,128)(2,1)} %bitcast.19, ...), custom_call_target="tpu_custom_call" | custom-call | tf_op jit(solution)/shard_map/pallas_call | solution.py:482

commit v3 on v2

--- a/solution.py
+++ b/solution.py
@@ -8,7 +8,8 @@
 from jax.sharding import PartitionSpec as P
 
 ROWS = 16
-LAG = 10
+LAG = 11
+LAST_FINE = 2
 EPSILON = 1e-05
 MESH = pl.DeviceIdType.MESH
 
@@ -72,8 +73,8 @@
     chips = replicas // 2
     quarter = half // 4
     pieces = ((0, quarter), (quarter, 2 * quarter), (3 * quarter, quarter))
-    take = ((0, 3),)
-    give = ((0, 3),)
+    take = {True: ((0, 2), (2, 3)), False: ((0, 3),)}
+    give = {True: ((0, 1), (1, 3)), False: ((0, 3),)}
     piece_of = [
         [k for k, (start, size) in enumerate(pieces) if start <= j * block < start + size][0]
         for j in range(chips)
@@ -290,18 +291,20 @@
                 src.at[i, :, part(chip)], dst.at[me, i // 2], x_recv.at[kind]
             ).start()
 
-    def forward_in(i):
+    def forward_in(i, fine):
         total = jnp.zeros((ROWS, 1), jnp.float32)
         u = jnp.zeros((ROWS, hidden), jnp.float32)
-        for first, past in take:
+        for first, past in take[fine]:
             start, stop = span(first, past)
             arrived(stash, f_recv, i, first, past)
 
-            @pl.when((i == 0) & is_first)
-            def _():
-                for j in range(chips):
-                    if start <= j * block < stop:
-                        wcopy(0, j).wait()
+            if fine:
+
+                @pl.when((i == 0) & is_first)
+                def _():
+                    for j in range(chips):
+                        if start <= j * block < stop:
+                            wcopy(0, j).wait()
 
             h = stash[i, :, start:stop].astype(jnp.float32)
             scaled = (h * gain[:, start:stop]).astype(jnp.bfloat16)
@@ -319,7 +322,7 @@
         def _():
             share(0, i, lambda j: stash.at[i, :, part(j)], all_h)
 
-    def forward_out(i):
+    def forward_out(i, fine):
         pltpu.make_async_copy(fx_recv.at[i], fx_recv.at[i], fx_sem.at[i]).wait()
         total = fx_send[i, :, hidden:] + fx_recv[i, :, hidden:]
         inv = lax.rsqrt(total / width + EPSILON)
@@ -329,13 +332,15 @@
         pre[i] = u
         act_buf[i] = act
 
-        @pl.when((i == 0) & is_first)
-        def _():
-            for j in range(chips):
-                wcopy(1, j).wait()
+        if fine:
+
+            @pl.when((i == 0) & is_first)
+            def _():
+                for j in range(chips):
+                    wcopy(1, j).wait()
 
         def emit(product):
-            for first, past in give:
+            for first, past in give[fine]:
                 start, stop = span(first, past)
                 h = stash[i, :, start:stop].astype(jnp.float32)
                 out_f[i, :, start:stop] = (h + product(act, start, stop)).astype(
@@ -344,9 +349,11 @@
                 for k in range(first, past):
                     send_forward(i, k).start()
 
-        @pl.when(is_first)
-        def _():
-            emit(lambda a, start, stop: nt_dot(a, wout[start:stop, :]))
+        if fine:
+
+            @pl.when(is_first)
+            def _():
+                emit(lambda a, start, stop: nt_dot(a, wout[start:stop, :]))
 
         @pl.when(not_first & not_last)
         def _():
@@ -354,9 +361,9 @@
 
         share(1, i, lambda j: act_buf.at[i], all_act)
 
-    def backward_in(i):
+    def backward_in(i, fine):
         da = jnp.zeros((ROWS, hidden), jnp.float32)
-        for first, past in take:
+        for first, past in take[fine]:
             start, stop = span(first, past)
             arrived(up, b_recv, i, first, past)
             da = da + dot(up[i, :, start:stop], wout[start:stop, :])
@@ -371,7 +378,7 @@
         def _():
             share(2, i, lambda j: up.at[i, :, part(j)], all_g)
 
-    def backward_out(i):
+    def backward_out(i, fine):
         pltpu.make_async_copy(bx_recv.at[i], bx_recv.at[i], bx_sem.at[i]).wait()
         da = bx_send[i] + bx_recv[i]
         u = pre[i]
@@ -387,7 +394,7 @@
                 inv * width
             )
             pull = inv * inv * inv * centered
-            for first, past in give:
+            for first, past in give[fine]:
                 start, stop = span(first, past)
                 h = stash[i, :, start:stop].astype(jnp.float32)
                 g = up[i, :, start:stop].astype(jnp.float32)
@@ -401,28 +408,40 @@
         share(3, i, lambda j: du_buf.at[i], all_du)
 
     lag = jnp.minimum(LAG * (sections - 1 - pos) // 2, count)
+    lag = jnp.where(is_first, count, lag)
     lead = is_first.astype(jnp.int32)
 
-    @pl.loop(0, count + lag + lead)
+    @pl.loop(0, count + lag)
     def _(step):
         ahead = step - lead
         back = step - lag
-
-        @pl.when(step < count)
-        def _():
-            forward_in(step)
-
-        @pl.when((back >= 0) & (back < count))
-        def _():
-            backward_in(back)
-
-        @pl.when((ahead >= 0) & (ahead < count))
-        def _():
-            forward_out(ahead)
-
-        @pl.when((back >= 0) & (back < count))
-        def _():
-            backward_out(back)
+        both = (back >= 0) & (step < count)
+        last = (step >= count) & (back >= count - LAST_FINE)
+
+        @pl.when(both)
+        def _():
+            forward_in(step, False)
+            backward_in(back, False)
+            forward_out(step, False)
+            backward_out(back, False)
+
+        @pl.when((step < count) & (back < 0))
+        def _():
+            forward_in(step, True)
+
+        @pl.when((ahead >= 0) & (ahead < count) & (ahead < lag))
+        def _():
+            forward_out(ahead, True)
+
+        @pl.when((step >= count) & jnp.logical_not(last))
+        def _():
+            backward_in(back, False)
+            backward_out(back, False)
+
+        @pl.when(last)
+        def _():
+            backward_in(back, True)
+            backward_out(back, True)
 
     @pl.loop(0, count)
     def _(i):
@@ -499,7 +518,7 @@
             jax.ShapeDtypeStruct((block, hidden), jnp.float32),
             jax.ShapeDtypeStruct((1, block), jnp.float32),
         ),
-        compiler_params=pltpu.CompilerParams(vmem_limit_bytes=62 * 2**20),
+        compiler_params=pltpu.CompilerParams(vmem_limit_bytes=40 * 2**20),
     )(me, h, g, act, du, weight_in, gains)
 
 
@@ -554,7 +573,7 @@
             dma((4,)),
         ],
         compiler_params=pltpu.CompilerParams(
-            collective_id=0, has_side_effects=True, vmem_limit_bytes=62 * 2**20
+            collective_id=0, has_side_effects=True, vmem_limit_bytes=44 * 2**20
         ),
     )(
         inputs.reshape(micros, ROWS, width),

time: 128 us -> 124 us (0.969)
  Pallas kernels: 128 us -> 123 us
    pallas_call x1, Pallas kernels: 120 us -> 117 us  [local(): pl.pallas_call(functools.partial(relay_kernel, sections, replicas, micros...]
    pallas_call x1, Pallas kernels: 7.72 us -> 5.95 us  [gradients(): pl.pallas_call(grad_kernel, grid_spec=pltpu.PrefetchScalarGridSpec(num_sc...]
where the time goes in v3:
time: 124 us
  Pallas kernels  123 us (99%)
    pallas_call x1, Pallas kernels, local(): pl.pallas_call(functools.partial(relay_kernel, sections, replicas, micros...  117 us
    pallas_call x1, Pallas kernels, gradients(): pl.pallas_call(grad_kernel, grid_spec=pltpu.PrefetchScalarGridSpec(num_sc...  5.95 us

profile of v3, /device:TPU:0, one launch (start us, length us, event | category | flops | bytes accessed | tf_op | source)
XLA Modules:
  0.0 123.9 jit_solution(2396906586283599640)
XLA Ops:
  0.6 0.0 copy-start
  0.6 0.7 copy-done
  1.4 116.6 %shard_map.76 = (bf16[8,10,16,1024]{3,2,1,0:T(8,128)(2,1)S(1)}, bf16[8,10,16,1024]{3,2,1,0:T(8,128)(2,1)S(1)}, bf16[8,10,16,512]{3,2,1,0:T(8,128)(2,1)S(1)}, bf16[8,10,16,512]{3,2,1,0:T(8,128)(2,1)S(1)}) custom-call(bf16[10,16,8192]{2,1,0:T(8,128)(2,1)} %bitcast.18, bf16[10,16,8192]{2,1,0:T(8,128)(2,1)} %bitcast.19, bf16[8192,512]{1,0:T(8,128)(2,1)} %bitcast.15, ...), custom_call_target="tpu_custom_call" | custom-call | tf_op jit(solution)/shard_map/pallas_call | solution.py:541
  118.0 5.9 %shard_map.77 = (f32[1024,512]{1,0:T(8,128)}, f32[1024,512]{1,0:T(8,128)}, f32[1,1024]{1,0:T(1,128)}) custom-call(s32[1]{0:T(128)} %bitcast.me_ref, bf16[1280,1024]{1,0:T(8,128)(2,1)S(1)} %bitcast.11, bf16[1280,1024]{1,0:T(8,128)(2,1)S(1)} %bitcast.12, bf16[1280,512]{1,0:T(8,128)(2,1)S(1)} %bitcast.13, bf16[1280,512]{1,0:T(8,128)(2,1)S(1)} %bitcast.14, ...), custom_call_target="tpu_custom_call" | custom-call | tf_op jit(solution)/shard_map/pallas_call | solution.py:501
Async XLA Ops:
  0.6 0.8 copy-start

commit v4 on v3

--- a/solution.py
+++ b/solution.py
@@ -10,6 +10,7 @@
 ROWS = 16
 LAG = 11
 LAST_FINE = 2
+EARLY = 2
 EPSILON = 1e-05
 MESH = pl.DeviceIdType.MESH
 
@@ -141,27 +142,6 @@
                 device_id_type=MESH,
             ).start()
 
-    @pl.when(is_first)
-    def _():
-        load_own(x_ref, stash, f_recv, 0)
-        load_weights(0)
-        load_weights(1)
-
-        @pl.loop(1, micros)
-        def _(m):
-            load_own(x_ref, stash, f_recv, m)
-
-    @pl.when(not_first)
-    def _():
-        load_weights(1)
-        load_weights(0)
-
-    @pl.when(is_last)
-    def _():
-        @pl.loop(0, micros)
-        def _(m):
-            load_own(c_ref, up, b_recv, m)
-
     barrier = pltpu.get_barrier_semaphore()
 
     @pl.when(not_first)
@@ -185,6 +165,27 @@
             device_id_type=MESH,
         )
 
+    @pl.when(is_first)
+    def _():
+        load_own(x_ref, stash, f_recv, 0)
+        load_weights(0)
+        load_weights(1)
+
+        @pl.loop(1, micros)
+        def _(m):
+            load_own(x_ref, stash, f_recv, m)
+
+    @pl.when(not_first)
+    def _():
+        load_weights(1)
+        load_weights(0)
+
+    @pl.when(is_last)
+    def _():
+        @pl.loop(0, micros)
+        def _(m):
+            load_own(c_ref, up, b_recv, m)
+
     for j in range(chips):
         gain[:, mine(j)] = gain_ref[:, part(2 * j + core)]
 
@@ -195,11 +196,9 @@
 
     @pl.when(is_first)
     def _():
-        @pl.loop(0, micros)
+        @pl.loop(0, EARLY)
         def _(m):
             push_partner(x_ref, stash, f_recv, m)
-
-        spread(x_ref, all_h, 0)
 
     @pl.when(is_last)
     def _():
@@ -429,6 +428,16 @@
         def _():
             forward_in(step, True)
 
+            later = step // 2 + EARLY
+
+            @pl.when(is_first & (lax.rem(step, 2) == 0) & (later < micros))
+            def _():
+                push_partner(x_ref, stash, f_recv, later)
+
+            @pl.when(is_first & (step == 1))
+            def _():
+                spread(x_ref, all_h, 0)
+
         @pl.when((ahead >= 0) & (ahead < count) & (ahead < lag))
         def _():
             forward_out(ahead, True)
@@ -493,7 +502,7 @@
 def gradients(me, h, g, act, du, weight_in, gains):
     total, block = h.shape
     hidden = act.shape[1]
-    rows = min(256, block)
+    rows = min(512, block)
     steps = block // rows
     tall = pl.BlockSpec((total, rows), lambda i, me_ref: (0, i))
     whole = pl.BlockSpec((total, hidden), lambda i, me_ref: (0, 0))

time: 124 us -> 124 us (level)
  no operation moved by 1% of the time
where the time goes in v4:
time: 124 us; the launch traced here: 123 us
  Pallas kernels  122 us (98%)
    pallas_call x1, Pallas kernels, local(): pl.pallas_call(functools.partial(relay_kernel, sections, replicas, micros...  117 us
    pallas_call x1, Pallas kernels, gradients(): pl.pallas_call(grad_kernel, grid_spec=pltpu.PrefetchScalarGridSpec(num_sc...  5.37 us

profile of v4, /device:TPU:0, one launch (start us, length us, event | category | flops | bytes accessed | tf_op | source)
XLA Modules:
  0.0 123.3 jit_solution(11318909325471889724)
XLA Ops:
  0.6 0.0 copy-start
  0.6 0.7 copy-done
  1.4 116.6 %shard_map.76 = (bf16[8,10,16,1024]{3,2,1,0:T(8,128)(2,1)S(1)}, bf16[8,10,16,1024]{3,2,1,0:T(8,128)(2,1)S(1)}, bf16[8,10,16,512]{3,2,1,0:T(8,128)(2,1)S(1)}, bf16[8,10,16,512]{3,2,1,0:T(8,128)(2,1)S(1)}) custom-call(bf16[10,16,8192]{2,1,0:T(8,128)(2,1)} %bitcast.18, bf16[10,16,8192]{2,1,0:T(8,128)(2,1)} %bitcast.19, bf16[8192,512]{1,0:T(8,128)(2,1)} %bitcast.15, ...), custom_call_target="tpu_custom_call" | custom-call | tf_op jit(solution)/shard_map/pallas_call | solution.py:550
  118.0 5.4 %shard_map.77 = (f32[1024,512]{1,0:T(8,128)}, f32[1024,512]{1,0:T(8,128)}, f32[1,1024]{1,0:T(1,128)}) custom-call(s32[1]{0:T(128)} %bitcast.me_ref, bf16[1280,1024]{1,0:T(8,128)(2,1)S(1)} %bitcast.11, bf16[1280,1024]{1,0:T(8,128)(2,1)S(1)} %bitcast.12, bf16[1280,512]{1,0:T(8,128)(2,1)S(1)} %bitcast.13, bf16[1280,512]{1,0:T(8,128)(2,1)S(1)} %bitcast.14, ...), custom_call_target="tpu_custom_call" | custom-call | tf_op jit(solution)/shard_map/pallas_call | solution.py:510
Async XLA Ops:
  0.6 0.8 copy-start

commit v5 on v4

--- a/solution.py
+++ b/solution.py
@@ -8,7 +8,7 @@
 from jax.sharding import PartitionSpec as P
 
 ROWS = 16
-LAG = 11
+LAG = 10
 LAST_FINE = 2
 EARLY = 2
 EPSILON = 1e-05
@@ -186,8 +186,13 @@
         def _(m):
             load_own(c_ref, up, b_recv, m)
 
+    def gain_copy(j):
+        return pltpu.make_async_copy(
+            gain_ref.at[:, part(2 * j + core)], gain.at[:, mine(j)], w_sem.at[2, j]
+        )
+
     for j in range(chips):
-        gain[:, mine(j)] = gain_ref[:, part(2 * j + core)]
+        gain_copy(j).start()
 
     pl.semaphore_wait(
         barrier,
@@ -220,6 +225,9 @@
         for j in range(chips):
             wcopy(0, j).wait()
             win_t[:, mine(j)] = win[mine(j), :].T
+
+    for j in range(chips):
+        gain_copy(j).wait()
 
     def send_forward(i, k):
         start, size = pieces[k]
@@ -410,6 +418,12 @@
     lag = jnp.where(is_first, count, lag)
     lead = is_first.astype(jnp.int32)
 
+    @pl.when(is_last)
+    def _():
+        @pl.loop(0, count)
+        def _(i):
+            backward_in(i, False)
+
     @pl.loop(0, count + lag)
     def _(step):
         ahead = step - lead
@@ -420,7 +434,11 @@
         @pl.when(both)
         def _():
             forward_in(step, False)
-            backward_in(back, False)
+
+            @pl.when(not_last)
+            def _():
+                backward_in(back, False)
+
             forward_out(step, False)
             backward_out(back, False)
 
@@ -541,7 +559,6 @@
     wide = jax.ShapeDtypeStruct((replicas, micros, ROWS, block), jnp.bfloat16)
     narrow = jax.ShapeDtypeStruct((replicas, micros, ROWS, hidden), jnp.bfloat16)
     any_spec = pl.BlockSpec(memory_space=pl.ANY)
-    vmem_spec = pl.BlockSpec(memory_space=pltpu.VMEM)
     wide_scratch = pltpu.VMEM((count, ROWS, half), jnp.bfloat16)
     narrow_scratch = pltpu.VMEM((count, ROWS, hidden), jnp.bfloat16)
     sums_scratch = pltpu.VMEM((count, ROWS, hidden + 128), jnp.float32)
@@ -550,7 +567,7 @@
     all_h, all_g, all_act, all_du = pl.pallas_call(
         functools.partial(relay_kernel, sections, replicas, micros),
         out_shape=(wide, wide, narrow, narrow),
-        in_specs=[any_spec] * 4 + [vmem_spec],
+        in_specs=[any_spec] * 5,
         out_specs=(any_spec,) * 4,
         scratch_shapes=[
             pltpu.VMEM((half, hidden), jnp.bfloat16),
@@ -570,7 +587,7 @@
             sums_scratch,
             rows_scratch,
             rows_scratch,
-            dma((2, replicas // 2)),
+            dma((3, replicas // 2)),
             dma((count, 3)),
             dma((count, 3)),
             dma((count, 3)),

time: 124 us -> 124 us (level)
  no operation moved by 1% of the time
where the time goes in v5:
time: 124 us; the launch traced here: 123 us
  Pallas kernels  122 us (98%)
    pallas_call x1, Pallas kernels, local(): pl.pallas_call(functools.partial(relay_kernel, sections, replicas, micros...  117 us
    pallas_call x1, Pallas kernels, gradients(): pl.pallas_call(grad_kernel, grid_spec=pltpu.PrefetchScalarGridSpec(num_sc...  5.36 us

profile of v5, /device:TPU:0, one launch (start us, length us, event | category | flops | bytes accessed | tf_op | source)
XLA Modules:
  0.0 123.3 jit_solution(6053323103020346769)
XLA Ops:
  0.6 0.0 copy-start
  0.6 0.7 copy-done
  1.4 116.6 %shard_map.76 = (bf16[8,10,16,1024]{3,2,1,0:T(8,128)(2,1)S(1)}, bf16[8,10,16,1024]{3,2,1,0:T(8,128)(2,1)S(1)}, bf16[8,10,16,512]{3,2,1,0:T(8,128)(2,1)S(1)}, bf16[8,10,16,512]{3,2,1,0:T(8,128)(2,1)S(1)}) custom-call(bf16[10,16,8192]{2,1,0:T(8,128)(2,1)} %bitcast.18, bf16[10,16,8192]{2,1,0:T(8,128)(2,1)} %bitcast.19, bf16[8192,512]{1,0:T(8,128)(2,1)} %bitcast.15, ...), custom_call_target="tpu_custom_call" | custom-call | tf_op jit(solution)/shard_map/pallas_call | solution.py:567
  118.0 5.4 %shard_map.77 = (f32[1024,512]{1,0:T(8,128)}, f32[1024,512]{1,0:T(8,128)}, f32[1,1024]{1,0:T(1,128)}) custom-call(s32[1]{0:T(128)} %bitcast.me_ref, bf16[1280,1024]{1,0:T(8,128)(2,1)S(1)} %bitcast.11, bf16[1280,1024]{1,0:T(8,128)(2,1)S(1)} %bitcast.12, bf16[1280,512]{1,0:T(8,128)(2,1)S(1)} %bitcast.13, bf16[1280,512]{1,0:T(8,128)(2,1)S(1)} %bitcast.14, ...), custom_call_target="tpu_custom_call" | custom-call | tf_op jit(solution)/shard_map/pallas_call | solution.py:528
Async XLA Ops:
  0.6 0.8 copy-start
